TPU v7x, 32 devices: a whole 2x2x4 slice. The times are simulated.
32 devices in a mesh: row: 8 (over z, x), col: 4 (over y, core).
Axes of the slice: x: 2, y: 2, z: 4, core: 2. Of those that a mesh axis runs over, the one named last changes fastest.
Arguments:
- pixels: bfloat16 [512, 512, 384], P('row', 'col'), may hold values from -40 to 40, as said below
- start: float32 [384, 64], replicated, may hold values from -0.3125 to 0.3125
Outputs:
- mean: float32 [384], replicated
- projector: float32 [384, 384], replicated
- scores: float32 [64, 512, 512], P(None, 'row', 'col')
Inputs may be any that keep to these rules, and one draw needn't show every extreme that they name: `pixels`: Real-valued features.
All inputs are finite; a program needn't handle non-finite values.
Results may differ from a plain program's by a relative error of at most 0.0029.
Values may be sent and summed in bfloat16 or wider, within the bound.
No kernel may reach another device: no remote copies, remote signals or barrier semaphores. Data moves between devices by JAX's collectives and lax.ppermute only.
A program may use at most 64 MiB of HBM per device.

v0:
```python
import jax
import jax.numpy as jnp
from jax import lax
from jax.sharding import PartitionSpec as P

ITERS = 4
GAUSS = (0.0625, 0.25, 0.375, 0.25, 0.0625)


def padded_2(shard, sides, width):
    for axis, dim in sides:
        size, length = (lax.axis_size(axis), shard.shape[dim])
        up = [(i, (i + 1) % size) for i in range(size - 1)]
        down = [(j, i) for i, j in up]
        last = lax.slice_in_dim(shard, length - width, length, axis=dim)
        first = lax.slice_in_dim(shard, 0, width, axis=dim)
        before = lax.ppermute(last, axis, up)
        after = lax.ppermute(first, axis, down)
        shard = jnp.concatenate([before, shard, after], axis=dim)
    return shard


def edge_weight(first, count, total):
    position = first + jnp.arange(count, dtype=jnp.int32)
    weight = jnp.zeros((count,), jnp.float32)
    for offset in range(5):
        inside = (position + offset - 2 >= 0) & (position + offset - 2 < total)
        weight = weight + GAUSS[offset] * inside.astype(jnp.float32)
    return weight


def along_rows(padded, count):
    total = GAUSS[0] * padded[0:count].astype(jnp.float32)
    for offset in range(1, 5):
        total = total + GAUSS[offset] * padded[offset : offset + count].astype(jnp.float32)
    return total


def along_cols(padded, count):
    total = GAUSS[0] * padded[:, 0:count]
    for offset in range(1, 5):
        total = total + GAUSS[offset] * padded[:, offset : offset + count]
    return total


def orthonormal(product):
    inner = jnp.dot(product.T, product, precision=lax.Precision.HIGHEST)
    lower_factor = jnp.linalg.cholesky(inner)
    return lax.linalg.triangular_solve(
        lower_factor, product, left_side=False, lower=True, transpose_a=True
    )


def local(pixels, start):
    tile_rows, tile_cols, feat = pixels.shape
    rows_total = tile_rows * lax.axis_size("row")
    cols_total = tile_cols * lax.axis_size("col")
    padded = padded_2(pixels, (("row", 0), ("col", 1)), 2)
    blurred = along_cols(along_rows(padded, tile_rows), tile_cols)
    row_weight = edge_weight(lax.axis_index("row") * tile_rows, tile_rows, rows_total)
    col_weight = edge_weight(lax.axis_index("col") * tile_cols, tile_cols, cols_total)
    weight = row_weight[:, None, None] * col_weight[None, :, None]
    smoothed = (blurred / weight).astype(jnp.bfloat16)
    flat = smoothed.reshape(tile_rows * tile_cols, feat)
    gram_local = lax.dot_general(
        flat, flat, (((0,), (0,)), ((), ())), preferred_element_type=jnp.float32
    )
    sums_local = jnp.sum(flat, axis=0, dtype=jnp.float32)
    count = float(rows_total * cols_total)
    basis = start
    gram, sums = lax.psum((gram_local, sums_local), ("row", "col"))
    mean = sums / count
    cov = gram / count - mean[:, None] * mean[None, :]
    for step in range(ITERS):
        basis = orthonormal(jnp.dot(cov, basis, precision=lax.Precision.HIGHEST))
    projector = jnp.dot(basis, basis.T, precision=lax.Precision.HIGHEST)
    basis_b = basis.astype(jnp.bfloat16)
    shift = jnp.dot(mean, basis_b.astype(jnp.float32), precision=lax.Precision.HIGHEST)
    scores = lax.dot_general(
        basis_b, flat, (((0,), (1,)), ((), ())), preferred_element_type=jnp.float32
    )
    scores = scores - shift[:, None]
    return (mean, projector, scores.reshape(basis.shape[1], tile_rows, tile_cols))


def solution(mesh):
    in_specs = (P("row", "col", None), P())
    out_specs = (P(), P(), P(None, "row", "col"))
    return jax.shard_map(local, mesh=mesh, in_specs=in_specs, out_specs=out_specs, check_vma=False)
```

profile of v0, /device:TPU:0, one launch (start us, length us, event | category | flops | bytes accessed | tf_op | source)
XLA Modules:
  0.0 266.5 jit_solution(16941923063009096975)
XLA Ops:
  8.3 4.9 %collective-permute-start = (bf16[2,128,384]{2,1,0:T(8,128)(2,1)S(1)}, bf16[2,128,384]{2,1,0:T(8,128)(2,1)S(1)}, u32[]{:S(2)}, u32[]{:S(2)}) collective-permute-start(bf16[2,128,384]{2,1,0:T(8,128)(2,1)S(1)} %get-tuple-element.10), channel_id=1, source_target_pairs={{0,4},{4,8},{8,12},{12,16},{16,20},{20,24},{24,28},{1,5},{5,9},{9,... | collective-permute-start | bytes 589832 | tf_op jit(solution)/shard_map/ppermute | solution.py:17
  14.5 2.9 %collective-permute-done = bf16[2,128,384]{2,1,0:T(8,128)(2,1)S(1)} collective-permute-done((bf16[2,128,384]{2,1,0:T(8,128)(2,1)S(1)}, bf16[2,128,384]{2,1,0:T(8,128)(2,1)S(1)}, u32[]{:S(2)}, u32[]{:S(2)}) %collective-permute-start) | collective-permute-done | bytes 196640 | tf_op jit(solution)/shard_map/ppermute | solution.py:17
  17.4 4.6 %constant_dynamic-update-slice_fusion.1 = bf16[68,128,384]{2,1,0:T(8,128)(2,1)S(1)} fusion(bf16[68,128,384]{2,1,0:T(8,128)(2,1)S(1)} %constant_dynamic-update-slice_fusion.2, bf16[64,128,384]{2,1,0:T(8,128)(2,1)} %param.5), kind=kLoop, calls=%fused_computation.56 | loop fusion | bytes 12582912
  24.9 3.6 %collective-permute-done.3 = bf16[68,2,384]{2,1,0:T(2,128)(2,1)S(1)} collective-permute-done((bf16[68,2,384]{2,1,0:T(2,128)(2,1)S(1)}, bf16[68,2,384]{2,1,0:T(2,128)(2,1)S(1)}, u32[]{:S(2)}, u32[]{:S(2)}) %collective-permute-start.3) | collective-permute-done | bytes 104480 | tf_op jit(solution)/shard_map/ppermute | solution.py:18
  28.5 3.6 %pad_maximum_fusion = bf16[68,132,384]{2,1,0:T(8,128)(2,1)S(1)} fusion(bf16[68,2,384]{2,1,0:T(2,128)(2,1)S(1)} %collective-permute-done.3, bf16[68,128,384]{2,1,0:T(8,128)(2,1)S(1)} %constant_dynamic-update-slice_fusion, bf16[68,2,384]{2,1,0:T(2,128)(2,1)S(1)} %collective-permute-done.2), kind=kLoop, calls=%fused_computation.14 | loop fusion | flops 20680704 | bytes 13787136 | tf_op jit(solution)/shard_map/concatenate | solution.py:19
  32.1 6.2 %multiply_add_fusion = f32[64,132,384]{2,1,0:T(8,128)S(1)} fusion(bf16[68,132,384]{2,1,0:T(8,128)(2,1)S(1)} %pad_maximum_fusion), kind=kLoop, calls=%fused_computation | loop fusion | flops 45416448 | bytes 45416448 | tf_op jit(solution)/shard_map/add | solution.py:35
  38.3 9.7 %convert_reduce_fusion = (f32[384]{0:T(512)S(1)}, bf16[64,128,384]{2,1,0:T(8,128)(2,1)}) fusion(f32[64,128]{1,0:T(8,128)S(1)} %broadcast_multiply_fusion, f32[64,132,384]{2,1,0:T(8,128)S(1)} %multiply_add_fusion), kind=kLoop, calls=%fused_computation.11 | loop fusion | flops 40894080 | bytes 69240320 | tf_op jit(solution)/shard_map/reduce_sum | solution.py:68
  48.1 8.8 %convolution_bitcast_fusion = f32[384,384]{1,0:T(8,128)} fusion(bf16[64,128,384]{2,1,0:T(8,128)(2,1)} %get-tuple-element.6), kind=kOutput, calls=%fused_computation.16 | convolution fusion | flops 2415919104 | bytes 6881280 | tf_op jit(solution)/shard_map/dot_general | solution.py:65
  56.9 47.5 %psum.14 = f32[384]{0:T(512)S(1)} all-reduce(f32[384]{0:T(512)S(1)} %get-tuple-element.5), channel_id=1, replica_groups=mesh['row'=8,'col'=4] {'row','col'}, use_global_device_ids=true, to_apply=%region_1.0 | all-reduce | flops 384 | bytes 3072 | tf_op jit(solution)/shard_map/psum | solution.py:71
  104.5 88.2 %all-reduce.2.cloned.1.call-done = f32[384,384]{1,0:T(8,128)} async-done(((f32[384,384]{1,0:T(8,128)}), f32[384,384]{1,0:T(8,128)}) %all-reduce.2.cloned.1.call-update) | async-done | bytes 589840 | tf_op jit(solution)/shard_map/psum | solution.py:71
  192.7 1.9 fusion.38
  195.0 5.8 %cholesky.74 = f32[64,64]{1,0:T(8,128)S(1)} custom-call(f32[64,64]{1,0:T(8,128)S(1)} %fusion.18), custom_call_target="Cholesky" | custom-call | tf_op jit(solution)/shard_map/jit(cholesky)/cholesky | solution.py:48
  202.2 4.9 %custom-call.8 = f32[1,64,64]{1,2,0:T(8,128)S(1)} custom-call(f32[1,64,64]{2,1,0:T(8,128)S(1)} %fusion.7), custom_call_target="InvertDiagBlocksLowerTriangular" | custom-call | tf_op jit(solution)/shard_map/triangular_solve/custom-call.0 | solution.py:49
  207.4 1.9 fusion.37
  209.7 5.8 %cholesky.85 = f32[64,64]{1,0:T(8,128)S(1)} custom-call(f32[64,64]{1,0:T(8,128)S(1)} %fusion.16), custom_call_target="Cholesky" | custom-call | tf_op jit(solution)/shard_map/jit(cholesky)/cholesky | solution.py:48
  216.9 4.9 %custom-call.9 = f32[1,64,64]{1,2,0:T(8,128)S(1)} custom-call(f32[1,64,64]{2,1,0:T(8,128)S(1)} %fusion.8), custom_call_target="InvertDiagBlocksLowerTriangular" | custom-call | tf_op jit(solution)/shard_map/triangular_solve/custom-call.0 | solution.py:49
  222.1 1.9 fusion.36
  224.4 5.8 %cholesky.96 = f32[64,64]{1,0:T(8,128)S(1)} custom-call(f32[64,64]{1,0:T(8,128)S(1)} %fusion.14), custom_call_target="Cholesky" | custom-call | tf_op jit(solution)/shard_map/jit(cholesky)/cholesky | solution.py:48
  231.6 4.9 %custom-call.10 = f32[1,64,64]{1,2,0:T(8,128)S(1)} custom-call(f32[1,64,64]{2,1,0:T(8,128)S(1)} %fusion.9), custom_call_target="InvertDiagBlocksLowerTriangular" | custom-call | tf_op jit(solution)/shard_map/triangular_solve/custom-call.0 | solution.py:49
  236.8 1.9 fusion.35
  239.1 5.8 %cholesky.107 = f32[64,64]{1,0:T(8,128)S(1)} custom-call(f32[64,64]{1,0:T(8,128)S(1)} %fusion.12), custom_call_target="Cholesky" | custom-call | tf_op jit(solution)/shard_map/jit(cholesky)/cholesky | solution.py:48
  246.2 4.9 %custom-call.11 = f32[1,64,64]{1,2,0:T(8,128)S(1)} custom-call(f32[1,64,64]{2,1,0:T(8,128)S(1)} %fusion.10), custom_call_target="InvertDiagBlocksLowerTriangular" | custom-call | tf_op jit(solution)/shard_map/triangular_solve/custom-call.0 | solution.py:49
  253.0 4.9 %fusion.6 = f32[8,8,64,128]{3,1,2,0:T(8,128)S(1)} fusion(bf16[8192,384]{1,0:T(8,128)(2,1)} %bitcast.74, f32[64]{0:T(128)S(1)} %convolution_bitcast_fusion.5, f32[384,64]{0,1:T(8,128)S(1)} %convolution_bitcast_fusion.1), kind=kOutput, calls=%fused_computation.15 | convolution fusion | flops 403202048 | bytes 8487168 | tf_op jit(solution)/shard_map/dot_general | solution.py:79
  258.0 1.7 copy.11
  (50 shorter events, 14.8 us)
Async XLA Ops:
  7.2 185.6 %copy-start = (f32[384,64]{0,1:T(8,128)S(1)}, f32[384,64]{0,1:T(8,128)}, u32[]{:S(2)}) copy-start(f32[384,64]{0,1:T(8,128)} %param.6) | copy-start | bytes 294916
  7.2 185.6 %all-reduce.2.cloned.1.call-start = ((), (), s32[]{:S(2)}) async-start(), calls=%async_computation | async-start | bytes 1179648 | tf_op jit(solution)/shard_map/psum | solution.py:71
  8.3 9.1 %collective-permute-start = (bf16[2,128,384]{2,1,0:T(8,128)(2,1)S(1)}, bf16[2,128,384]{2,1,0:T(8,128)(2,1)S(1)}, u32[]{:S(2)}, u32[]{:S(2)}) collective-permute-start(bf16[2,128,384]{2,1,0:T(8,128)(2,1)S(1)} %get-tuple-element.10), channel_id=1, source_target_pairs={{0,4},{4,8},{8,12},{12,16},{16,20},{20,24},{24,28},{1,5},{5,9},{9,... | collective-permute-start | bytes 589832 | tf_op jit(solution)/shard_map/ppermute | solution.py:17
  13.2 8.8 %collective-permute-start.1 = (bf16[2,128,384]{2,1,0:T(8,128)(2,1)S(1)}, bf16[2,128,384]{2,1,0:T(8,128)(2,1)S(1)}, u32[]{:S(2)}, u32[]{:S(2)}) collective-permute-start(bf16[2,128,384]{2,1,0:T(8,128)(2,1)S(1)} %get-tuple-element.9), channel_id=1, source_target_pairs={{4,0},{8,4},{12,8},{16,12},{20,16},{24,20},{28,24},{5,1},{9,5},{13... | collective-permute-start | bytes 589832 | tf_op jit(solution)/shard_map/ppermute | solution.py:18
  22.2 2.7 %collective-permute-start.2 = (bf16[68,2,384]{2,1,0:T(2,128)(2,1)S(1)}, bf16[68,2,384]{2,1,0:T(2,128)(2,1)S(1)}, u32[]{:S(2)}, u32[]{:S(2)}) collective-permute-start(bf16[68,2,384]{2,1,0:T(2,128)(2,1)S(1)} %get-tuple-element.7), channel_id=1, source_target_pairs={{0,1},{1,2},{2,3},{4,5},{5,6},{6,7},{8,9},{9,10},{10,11},{12,13},{... | collective-permute-start | bytes 313352 | tf_op jit(solution)/shard_map/ppermute | solution.py:17
  23.5 5.0 %collective-permute-start.3 = (bf16[68,2,384]{2,1,0:T(2,128)(2,1)S(1)}, bf16[68,2,384]{2,1,0:T(2,128)(2,1)S(1)}, u32[]{:S(2)}, u32[]{:S(2)}) collective-permute-start(bf16[68,2,384]{2,1,0:T(2,128)(2,1)S(1)} %get-tuple-element.8), channel_id=1, source_target_pairs={{1,0},{2,1},{3,2},{5,4},{6,5},{7,6},{9,8},{10,9},{11,10},{13,12},{... | collective-permute-start | bytes 313352 | tf_op jit(solution)/shard_map/ppermute | solution.py:18
  104.5 155.2 %copy-start.1 = (f32[384]{0:T(512)}, f32[384]{0:T(512)S(1)}, u32[]{:S(2)}) copy-start(f32[384]{0:T(512)S(1)} %broadcast_multiply_fusion.1) | copy-start | bytes 4612
Sparse Core Ops, SparseCore 0:
  57.0 135.6 all-reduce.1
where the time goes:
time: 267 us
  waiting for transfers between devices  94.7 us (35%)
  other arithmetic  68 us (25%)
  blocking collectives  47.5 us (18%)
  matrix products  25.3 us (9%)
  between operations  14.4 us (5%)
  starting transfers between devices  8.8 us (3%)
  local copies, waits for them, and re-layouts  7.87 us (3%)
    psum x1, waiting for transfers between devices, local(): gram, sums = lax.psum((gram_local, sums_local), ('row', 'col'))  88.2 us
    psum x1, blocking collectives, local(): gram, sums = lax.psum((gram_local, sums_local), ('row', 'col'))  47.5 us
    another operation x12, other arithmetic, orthonormal(): lower_factor = jnp.linalg.cholesky(inner)  26.1 us
    another operation x8, other arithmetic, orthonormal(): lax.linalg.triangular_solve(lower_factor, product, left_side=False, lower...  22.2 us
    reduce_sum x1, other arithmetic, local(): sums_local = jnp.sum(flat, axis=0, dtype=jnp.float32)  9.75 us
    dot_general x1, matrix products, local(): lax.dot_general(flat, flat, (((0,), (0,)), ((), ())), preferred_element_t...  8.85 us
    dot_general x4, matrix products, local(): basis = orthonormal(jnp.dot(cov, basis, precision=lax.Precision.HIGHEST))  7.72 us
    unnamed x7, local copies, waits for them, and re-layouts  6.31 us
  transfers between devices with their start and end apart: 5, of which 3 were waited for; matrix products, arithmetic and copies ran while one was open for 2% of the time, Pallas kernels for 0%

commit v1 on v0

--- a/solution.py
+++ b/solution.py
@@ -5,6 +5,9 @@
 
 ITERS = 4
 GAUSS = (0.0625, 0.25, 0.375, 0.25, 0.0625)
+_replace_sites = lambda row_data, bus_axis, along_axis: jax.lax.psum(
+    jax.lax.psum(row_data, bus_axis), along_axis
+)
 
 
 def padded_2(shard, sides, width):
@@ -68,7 +71,7 @@
     sums_local = jnp.sum(flat, axis=0, dtype=jnp.float32)
     count = float(rows_total * cols_total)
     basis = start
-    gram, sums = lax.psum((gram_local, sums_local), ("row", "col"))
+    gram, sums = _replace_sites((gram_local, sums_local), "col", "row")
     mean = sums / count
     cov = gram / count - mean[:, None] * mean[None, :]
     for step in range(ITERS):

time: 267 us -> 249 us (0.933)
  blocking collectives: 47.5 us -> 27.4 us
    psum x1 -> x2, blocking collectives: 47.5 us -> 27.4 us  [the longest x1 21.6 us: jax.lax.psum(jax.lax.psum(row_data, bus_axis), along_axis)]
    psum x1 -> x2, waiting for transfers between devices: 88.2 us -> 90.6 us  [the longest x1 49.4 us: jax.lax.psum(jax.lax.psum(row_data, bus_axis), along_axis)]
  transfers between devices with their start and end apart: 5 -> 6, of which waited for: 3 -> 4; matrix products, arithmetic and copies ran while one was open for 2% -> 2% of each run, Pallas kernels for 0% -> 0%
where the time goes in v1:
time: 249 us
  waiting for transfers between devices  97.1 us (39%)
  other arithmetic  68 us (27%)
  blocking collectives  27.4 us (11%)
  matrix products  25.3 us (10%)
  between operations  14.4 us (6%)
  starting transfers between devices  8.84 us (4%)
  local copies, waits for them, and re-layouts  7.87 us (3%)
    psum x1, waiting for transfers between devices, jax.lax.psum(jax.lax.psum(row_data, bus_axis), along_axis)  49.4 us
    psum x1, waiting for transfers between devices, jax.lax.psum(row_data, bus_axis)  41.2 us
    another operation x12, other arithmetic, orthonormal(): lower_factor = jnp.linalg.cholesky(inner)  26.1 us
    another operation x8, other arithmetic, orthonormal(): lax.linalg.triangular_solve(lower_factor, product, left_side=False, lower...  22.2 us
    psum x1, blocking collectives, jax.lax.psum(jax.lax.psum(row_data, bus_axis), along_axis)  21.6 us
    reduce_sum x1, other arithmetic, local(): sums_local = jnp.sum(flat, axis=0, dtype=jnp.float32)  9.75 us
    dot_general x1, matrix products, local(): lax.dot_general(flat, flat, (((0,), (0,)), ((), ())), preferred_element_t...  8.85 us
    dot_general x4, matrix products, local(): basis = orthonormal(jnp.dot(cov, basis, precision=lax.Precision.HIGHEST))  7.72 us
  transfers between devices with their start and end apart: 6, of which 4 were waited for; matrix products, arithmetic and copies ran while one was open for 2% of the time, Pallas kernels for 0%

profile of v1, /device:TPU:0, one launch (start us, length us, event | category | flops | bytes accessed | tf_op | source)
XLA Modules:
  0.0 248.8 jit_solution(418254963578413365)
XLA Ops:
  8.3 4.9 %collective-permute-start = (bf16[2,128,384]{2,1,0:T(8,128)(2,1)S(1)}, bf16[2,128,384]{2,1,0:T(8,128)(2,1)S(1)}, u32[]{:S(2)}, u32[]{:S(2)}) collective-permute-start(bf16[2,128,384]{2,1,0:T(8,128)(2,1)S(1)} %get-tuple-element.10), channel_id=1, source_target_pairs={{0,4},{4,8},{8,12},{12,16},{16,20},{20,24},{24,28},{1,5},{5,9},{9,... | collective-permute-start | bytes 589832 | tf_op jit(solution)/shard_map/ppermute | solution.py:20
  14.5 2.9 %collective-permute-done = bf16[2,128,384]{2,1,0:T(8,128)(2,1)S(1)} collective-permute-done((bf16[2,128,384]{2,1,0:T(8,128)(2,1)S(1)}, bf16[2,128,384]{2,1,0:T(8,128)(2,1)S(1)}, u32[]{:S(2)}, u32[]{:S(2)}) %collective-permute-start) | collective-permute-done | bytes 196640 | tf_op jit(solution)/shard_map/ppermute | solution.py:20
  17.4 4.6 %constant_dynamic-update-slice_fusion.1 = bf16[68,128,384]{2,1,0:T(8,128)(2,1)S(1)} fusion(bf16[68,128,384]{2,1,0:T(8,128)(2,1)S(1)} %constant_dynamic-update-slice_fusion.2, bf16[64,128,384]{2,1,0:T(8,128)(2,1)} %param.5), kind=kLoop, calls=%fused_computation.56 | loop fusion | bytes 12582912
  24.9 3.6 %collective-permute-done.3 = bf16[68,2,384]{2,1,0:T(2,128)(2,1)S(1)} collective-permute-done((bf16[68,2,384]{2,1,0:T(2,128)(2,1)S(1)}, bf16[68,2,384]{2,1,0:T(2,128)(2,1)S(1)}, u32[]{:S(2)}, u32[]{:S(2)}) %collective-permute-start.3) | collective-permute-done | bytes 104480 | tf_op jit(solution)/shard_map/ppermute | solution.py:21
  28.5 3.6 %pad_maximum_fusion = bf16[68,132,384]{2,1,0:T(8,128)(2,1)S(1)} fusion(bf16[68,2,384]{2,1,0:T(2,128)(2,1)S(1)} %collective-permute-done.3, bf16[68,128,384]{2,1,0:T(8,128)(2,1)S(1)} %constant_dynamic-update-slice_fusion, bf16[68,2,384]{2,1,0:T(2,128)(2,1)S(1)} %collective-permute-done.2), kind=kLoop, calls=%fused_computation.14 | loop fusion | flops 20680704 | bytes 13787136 | tf_op jit(solution)/shard_map/concatenate | solution.py:22
  32.1 6.2 %multiply_add_fusion = f32[64,132,384]{2,1,0:T(8,128)S(1)} fusion(bf16[68,132,384]{2,1,0:T(8,128)(2,1)S(1)} %pad_maximum_fusion), kind=kLoop, calls=%fused_computation | loop fusion | flops 45416448 | bytes 45416448 | tf_op jit(solution)/shard_map/add | solution.py:38
  38.3 9.7 %convert_reduce_fusion = (f32[384]{0:T(512)S(1)}, bf16[64,128,384]{2,1,0:T(8,128)(2,1)}) fusion(f32[64,128]{1,0:T(8,128)S(1)} %broadcast_multiply_fusion, f32[64,132,384]{2,1,0:T(8,128)S(1)} %multiply_add_fusion), kind=kLoop, calls=%fused_computation.11 | loop fusion | flops 40894080 | bytes 69240320 | tf_op jit(solution)/shard_map/reduce_sum | solution.py:71
  48.1 8.8 %convolution_bitcast_fusion = f32[384,384]{1,0:T(8,128)} fusion(bf16[64,128,384]{2,1,0:T(8,128)(2,1)} %get-tuple-element.6), kind=kOutput, calls=%fused_computation.16 | convolution fusion | flops 2415919104 | bytes 6881280 | tf_op jit(solution)/shard_map/dot_general | solution.py:68
  57.0 41.2 %all-reduce.3.cloned.1.call-done = f32[384,384]{1,0:T(8,128)} async-done(((f32[384,384]{1,0:T(8,128)}), f32[384,384]{1,0:T(8,128)}) %all-reduce.3.cloned.1.call-update) | async-done | bytes 589840 | tf_op jit(solution)/shard_map/psum | solution.py:9
  98.2 5.8 %psum.28 = f32[384]{0:T(512)S(1)} all-reduce(f32[384]{0:T(512)S(1)} %get-tuple-element.5), channel_id=1, replica_groups=mesh['row'=8,'col'=4] {'col'}, use_global_device_ids=true, to_apply=%region_1.0 | all-reduce | flops 384 | bytes 3072 | tf_op jit(solution)/shard_map/psum | solution.py:9
  104.0 21.6 %psum.29 = f32[384]{0:T(512)S(1)} all-reduce(f32[384]{0:T(512)S(1)} %psum.28), channel_id=1, replica_groups=mesh['row'=8,'col'=4] {'row'}, use_global_device_ids=true, to_apply=%region_2.0 | all-reduce | flops 384 | bytes 3072 | tf_op jit(solution)/shard_map/psum | solution.py:8
  125.6 49.4 %all-reduce.5.cloned.1.call-done = f32[384,384]{1,0:T(8,128)} async-done(((f32[384,384]{1,0:T(8,128)}), f32[384,384]{1,0:T(8,128)}) %all-reduce.5.cloned.1.call-update) | async-done | bytes 589840 | tf_op jit(solution)/shard_map/psum | solution.py:8
  177.3 5.8 %cholesky.74 = f32[64,64]{1,0:T(8,128)S(1)} custom-call(f32[64,64]{1,0:T(8,128)S(1)} %fusion.18), custom_call_target="Cholesky" | custom-call | tf_op jit(solution)/shard_map/jit(cholesky)/cholesky | solution.py:51
  184.5 4.9 %custom-call.8 = f32[1,64,64]{1,2,0:T(8,128)S(1)} custom-call(f32[1,64,64]{2,1,0:T(8,128)S(1)} %fusion.7), custom_call_target="InvertDiagBlocksLowerTriangular" | custom-call | tf_op jit(solution)/shard_map/triangular_solve/custom-call.0 | solution.py:52
  189.7 1.9 fusion.37
  192.0 5.8 %cholesky.85 = f32[64,64]{1,0:T(8,128)S(1)} custom-call(f32[64,64]{1,0:T(8,128)S(1)} %fusion.16), custom_call_target="Cholesky" | custom-call | tf_op jit(solution)/shard_map/jit(cholesky)/cholesky | solution.py:51
  199.1 4.9 %custom-call.9 = f32[1,64,64]{1,2,0:T(8,128)S(1)} custom-call(f32[1,64,64]{2,1,0:T(8,128)S(1)} %fusion.8), custom_call_target="InvertDiagBlocksLowerTriangular" | custom-call | tf_op jit(solution)/shard_map/triangular_solve/custom-call.0 | solution.py:52
  204.3 1.9 fusion.36
  206.6 5.8 %cholesky.96 = f32[64,64]{1,0:T(8,128)S(1)} custom-call(f32[64,64]{1,0:T(8,128)S(1)} %fusion.14), custom_call_target="Cholesky" | custom-call | tf_op jit(solution)/shard_map/jit(cholesky)/cholesky | solution.py:51
  213.8 4.9 %custom-call.10 = f32[1,64,64]{1,2,0:T(8,128)S(1)} custom-call(f32[1,64,64]{2,1,0:T(8,128)S(1)} %fusion.9), custom_call_target="InvertDiagBlocksLowerTriangular" | custom-call | tf_op jit(solution)/shard_map/triangular_solve/custom-call.0 | solution.py:52
  219.0 1.9 fusion.35
  221.3 5.8 %cholesky.107 = f32[64,64]{1,0:T(8,128)S(1)} custom-call(f32[64,64]{1,0:T(8,128)S(1)} %fusion.12), custom_call_target="Cholesky" | custom-call | tf_op jit(solution)/shard_map/jit(cholesky)/cholesky | solution.py:51
  228.5 4.9 %custom-call.11 = f32[1,64,64]{1,2,0:T(8,128)S(1)} custom-call(f32[1,64,64]{2,1,0:T(8,128)S(1)} %fusion.10), custom_call_target="InvertDiagBlocksLowerTriangular" | custom-call | tf_op jit(solution)/shard_map/triangular_solve/custom-call.0 | solution.py:52
  235.3 4.9 %fusion.6 = f32[8,8,64,128]{3,1,2,0:T(8,128)S(1)} fusion(bf16[8192,384]{1,0:T(8,128)(2,1)} %bitcast.74, f32[64]{0:T(128)S(1)} %convolution_bitcast_fusion.5, f32[384,64]{0,1:T(8,128)S(1)} %convolution_bitcast_fusion.1), kind=kOutput, calls=%fused_computation.15 | convolution fusion | flops 403202048 | bytes 8487168 | tf_op jit(solution)/shard_map/dot_general | solution.py:82
  (54 shorter events, 18.5 us)
Async XLA Ops:
  7.2 167.8 %copy-start = (f32[384,64]{0,1:T(8,128)S(1)}, f32[384,64]{0,1:T(8,128)}, u32[]{:S(2)}) copy-start(f32[384,64]{0,1:T(8,128)} %param.6) | copy-start | bytes 294916
  7.2 91.0 %all-reduce.3.cloned.1.call-start = ((), (), s32[]{:S(2)}) async-start(), calls=%async_computation | async-start | bytes 1179648 | tf_op jit(solution)/shard_map/psum | solution.py:9
  8.3 9.1 %collective-permute-start = (bf16[2,128,384]{2,1,0:T(8,128)(2,1)S(1)}, bf16[2,128,384]{2,1,0:T(8,128)(2,1)S(1)}, u32[]{:S(2)}, u32[]{:S(2)}) collective-permute-start(bf16[2,128,384]{2,1,0:T(8,128)(2,1)S(1)} %get-tuple-element.10), channel_id=1, source_target_pairs={{0,4},{4,8},{8,12},{12,16},{16,20},{20,24},{24,28},{1,5},{5,9},{9,... | collective-permute-start | bytes 589832 | tf_op jit(solution)/shard_map/ppermute | solution.py:20
  13.2 8.8 %collective-permute-start.1 = (bf16[2,128,384]{2,1,0:T(8,128)(2,1)S(1)}, bf16[2,128,384]{2,1,0:T(8,128)(2,1)S(1)}, u32[]{:S(2)}, u32[]{:S(2)}) collective-permute-start(bf16[2,128,384]{2,1,0:T(8,128)(2,1)S(1)} %get-tuple-element.9), channel_id=1, source_target_pairs={{4,0},{8,4},{12,8},{16,12},{20,16},{24,20},{28,24},{5,1},{9,5},{13... | collective-permute-start | bytes 589832 | tf_op jit(solution)/shard_map/ppermute | solution.py:21
  22.2 2.7 %collective-permute-start.2 = (bf16[68,2,384]{2,1,0:T(2,128)(2,1)S(1)}, bf16[68,2,384]{2,1,0:T(2,128)(2,1)S(1)}, u32[]{:S(2)}, u32[]{:S(2)}) collective-permute-start(bf16[68,2,384]{2,1,0:T(2,128)(2,1)S(1)} %get-tuple-element.7), channel_id=1, source_target_pairs={{0,1},{1,2},{2,3},{4,5},{5,6},{6,7},{8,9},{9,10},{10,11},{12,13},{... | collective-permute-start | bytes 313352 | tf_op jit(solution)/shard_map/ppermute | solution.py:20
  23.5 5.0 %collective-permute-start.3 = (bf16[68,2,384]{2,1,0:T(2,128)(2,1)S(1)}, bf16[68,2,384]{2,1,0:T(2,128)(2,1)S(1)}, u32[]{:S(2)}, u32[]{:S(2)}) collective-permute-start(bf16[68,2,384]{2,1,0:T(2,128)(2,1)S(1)} %get-tuple-element.8), channel_id=1, source_target_pairs={{1,0},{2,1},{3,2},{5,4},{6,5},{7,6},{9,8},{10,9},{11,10},{13,12},{... | collective-permute-start | bytes 313352 | tf_op jit(solution)/shard_map/ppermute | solution.py:21
  56.9 118.1 %all-reduce.5.cloned.1.call-start = ((), (), s32[]{:S(2)}) async-start(), calls=%async_computation.1 | async-start | bytes 1179648 | tf_op jit(solution)/shard_map/psum | solution.py:8
  125.6 116.4 %copy-start.1 = (f32[384]{0:T(512)}, f32[384]{0:T(512)S(1)}, u32[]{:S(2)}) copy-start(f32[384]{0:T(512)S(1)} %broadcast_multiply_fusion.1) | copy-start | bytes 4612
Sparse Core Ops, SparseCore 0:
  57.0 41.0 all-reduce.2
  101.6 73.3 all-reduce.4
